TPU v7x, 32 devices: a whole 2x2x4 slice. The times are simulated.
32 devices in a mesh: gx: 8 (over z, y), gy: 4 (over x, core).
Axes of the slice: x: 2, y: 2, z: 4, core: 2. Of those that a mesh axis runs over, the one named last changes fastest.
Arguments:
- fuel: float32 [16, 768, 384], P('gx', 'gy'), may hold values from -41 to 41, as said below
- oxidizer: float32 [16, 768, 384], P('gx', 'gy'), may hold values from -41 to 41, as said below
- kappa: float32 [16, 768, 384], P('gx', 'gy'), may hold values from 0.05 to 0.5
- rate: float32 [16, 768, 384], P('gx', 'gy'), may hold values from 0.5 to 5
Outputs:
- fuel_next: float32 [16, 768, 384], P('gx', 'gy')
- oxid_next: float32 [16, 768, 384], P('gx', 'gy')
- r_factor: float32 [384, 384], replicated
Inputs may be any that keep to these rules, and one draw needn't show every extreme that they name: `fuel`: A real-valued field. `oxidizer`: A real-valued field.
All inputs are finite; a program needn't handle non-finite values.
Results may differ from a plain program's by a relative error of at most 0.000067.
Values sent between devices are 32-bit elements; how exact they have to be, the bound alone decides.
A program may use at most 64 MiB of HBM per device.

v0:
```python
import functools

import jax
import jax.numpy as jnp
from jax import lax
from jax.experimental import pallas as pl
from jax.experimental.pallas import tpu as pltpu
from jax.sharding import PartitionSpec as P

MESH = pl.DeviceIdType.MESH
TILE = 8
LANES = 128
HIGHEST = lax.Precision.HIGHEST


def peer(index, stage, k):
    axis, stride, size = stage
    mine = lax.rem(index[axis] // stride, size)
    other = lax.rem(mine + k, size)
    place = dict(index)
    place[axis] = index[axis] + (other - mine) * stride
    return mine, other, (place["gx"], place["gy"])


def sum_over_all(index, stages, source, out_ref, inbox, held, sems):
    count = len(stages)
    length = source.shape[0]
    starts = []
    start = 0
    for s, stage in enumerate(stages):
        size = stage[2]
        length //= size
        sent = []
        for k in range(1, size):
            mine, other, device = peer(index, stage, k)
            sent.append(
                pltpu.make_async_remote_copy(
                    src_ref=source.at[pl.ds(pl.multiple_of(other * length, TILE), length)],
                    dst_ref=inbox[s].at[k - 1],
                    send_sem=sems[0].at[s, k - 1],
                    recv_sem=sems[1].at[s, k - 1],
                    device_id=device,
                    device_id_type=MESH,
                )
            )
            sent[-1].start()
        for copy in sent:
            copy.wait_recv()
        total = source[pl.ds(pl.multiple_of(mine * length, TILE), length)]
        for k in range(1, size):
            total = total + inbox[s][k - 1]
        held[s][...] = total
        for copy in sent:
            copy.wait_send()
        source = held[s]
        start = start + mine * length
        starts.append((start, length))
    part = pl.ds(pl.multiple_of(start, TILE), length)
    out_ref[part] = source[...]
    for s in reversed(range(count)):
        start, length = starts[s]
        part = pl.ds(pl.multiple_of(start, TILE), length)
        sent = []
        for k in range(1, stages[s][2]):
            sent.append(
                pltpu.make_async_remote_copy(
                    src_ref=out_ref.at[part],
                    dst_ref=out_ref.at[part],
                    send_sem=sems[2].at[s, k - 1],
                    recv_sem=sems[3].at[s, k - 1],
                    device_id=peer(index, stages[s], k)[2],
                    device_id_type=MESH,
                )
            )
            sent[-1].start()
        for copy in sent:
            copy.wait()


def update_kernel(
    n, m, rows, parts, stages,
    f_hbm, o_hbm, k_hbm, r_hbm, fn_hbm, on_hbm, g_out,
    f_ref, o_ref, k_ref, r_ref, fn_ref, on_ref, xlo, xhi, ylo, yhi, gram, passing,
    local_sem, xs_sem, xr_sem, ys_sem, yr_sem, ps_sem, pr_sem, *scratch
):
    i, j = lax.axis_index("gx"), lax.axis_index("gy")
    index = {"gx": i, "gy": j}
    planes, width, depth = f_ref.shape
    step = width // parts
    sides = (
        (i < n - 1, i > 0, i + 1, j),
        (i > 0, i < n - 1, i - 1, j),
        (j < m - 1, j > 0, i, j + 1),
        (j > 0, j < m - 1, i, j - 1),
    )
    z, odd, depth_z = i // 2, lax.rem(i, 2) == 1, n // 2
    rising = lambda pair: (pair + 1) * parts // depth_z
    falling = lambda pair: (depth_z - 1 - pair) * parts // depth_z
    if n % 2 or n < 4:
        indirect = (0, 0)
        relayed = 0
    else:
        indirect = (jnp.where(odd, falling(z), 0), jnp.where(odd, 0, rising(z - 1)))
        relayed = jnp.where(odd, rising(z - 1), falling(z))
    via = (i - 1, i + 1)
    onward = jnp.where(odd, i - 2, i + 2)
    lands = (jnp.logical_not(odd), odd)
    relayed = jnp.where(odd, jnp.where(z > 0, relayed, 0), jnp.where(z < depth_z - 1, relayed, 0))
    greets = sides + ((i < n - 2, None, i + 2, j), (i > 1, None, i - 2, j))
    barrier = pltpu.get_barrier_semaphore()
    greeted = sum(has.astype(jnp.int32) for has, _, _, _ in greets)
    for has, _, a, b in greets:
        @pl.when(has)
        def _(a=a, b=b):
            pl.semaphore_signal(barrier, inc=1, device_id=(a, b), device_id_type=MESH)
    for stage in stages:
        for k in range(1, stage[2]):
            pl.semaphore_signal(barrier, inc=1, device_id=peer(index, stage, k)[2], device_id_type=MESH)
            greeted = greeted + 1
    pl.semaphore_wait(barrier, greeted)
    fields = (f_hbm, o_hbm, k_hbm)

    def x_copies(side, part):
        _, _, a, b = sides[side]
        cut = pl.ds(part * step, step)
        return [
            pltpu.make_async_remote_copy(
                src_ref=ref.at[(planes - 1, 0)[side], cut],
                dst_ref=(xlo, xhi)[side].at[t, cut],
                send_sem=xs_sem.at[side, part, t],
                recv_sem=xr_sem.at[side, part, t],
                device_id=(a, b),
                device_id_type=MESH,
            )
            for t, ref in enumerate(fields)
        ]

    def to_relay(side, part):
        cut = pl.ds(part * step, step)
        return [
            pltpu.make_async_remote_copy(
                src_ref=ref.at[(planes - 1, 0)[side], cut],
                dst_ref=passing.at[t, cut],
                send_sem=xs_sem.at[side, part, t],
                recv_sem=pr_sem.at[part, t],
                device_id=(via[side], j),
                device_id_type=MESH,
            )
            for t, ref in enumerate(fields)
        ]

    def from_relay(side, part):
        cut = pl.ds(part * step, step)
        return [
            pltpu.make_async_remote_copy(
                src_ref=passing.at[t, cut],
                dst_ref=(xlo, xhi)[side].at[t, cut],
                send_sem=ps_sem.at[part, t],
                recv_sem=xr_sem.at[side, part, t],
                device_id=(onward, j),
                device_id_type=MESH,
            )
            for t in range(3)
        ]

    def y_copies(side):
        _, _, a, b = sides[2 + side]
        return [
            pltpu.make_async_remote_copy(
                src_ref=ref.at[:, pl.ds((width - TILE, 0)[side], TILE)],
                dst_ref=(ylo, yhi)[side].at[t],
                send_sem=ys_sem.at[side, t],
                recv_sem=yr_sem.at[side, t],
                device_id=(a, b),
                device_id_type=MESH,
            )
            for t, ref in enumerate(fields)
        ]

    for side in range(2):
        @pl.when(sides[2 + side][0])
        def _(side=side):
            for copy in y_copies(side):
                copy.start()
    for part in range(parts):
        for side in range(2):
            @pl.when(sides[side][0] & (part >= indirect[side]))
            def _(side=side, part=part):
                for copy in x_copies(side, part):
                    copy.start()

            @pl.when(sides[side][0] & (part < indirect[side]))
            def _(side=side, part=part):
                for copy in to_relay(side, part):
                    copy.start()
    loads = [
        pltpu.make_async_copy(src, dst, local_sem.at[t])
        for t, (src, dst) in enumerate(((f_hbm, f_ref), (o_hbm, o_ref), (k_hbm, k_ref), (r_hbm, r_ref)))
    ]
    for copy in loads:
        copy.start()
    for copy in loads:
        copy.wait()
    for side in range(2):
        @pl.when(sides[2 + side][1])
        def _(side=side):
            for copy in y_copies(side):
                copy.wait_recv()

    row = lax.broadcasted_iota(jnp.int32, (step, depth), 0)
    lane = lax.broadcasted_iota(jnp.int32, (step, depth), 1)
    refs = (f_ref, o_ref, k_ref)
    zero = jnp.zeros((step, depth), jnp.float32)
    zrow = jnp.zeros((1, depth), jnp.float32)
    dims = (((0,), (0,)), ((), ()))
    for q in range(parts):
        @pl.when(q < relayed)
        def _(q=q):
            for copy in to_relay(0, q):
                copy.wait_recv()

        for side in range(2):
            @pl.when((q < relayed) & lands[side])
            def _(side=side, q=q):
                for copy in from_relay(side, q):
                    copy.start()

        for side in range(2):
            @pl.when(sides[side][1])
            def _(side=side, q=q):
                for copy in x_copies(side, q):
                    copy.wait_recv()
        y = q * step
        part = pl.ds(y, step)
        for x in range(planes):
            center = [ref[x, part] for ref in refs]
            sets = []
            if x == 0:
                sets.append([jnp.where(i > 0, xlo[t, part], zero) for t in range(3)])
            else:
                sets.append([ref[x - 1, part] for ref in refs])
            if x == planes - 1:
                sets.append([jnp.where(i < n - 1, xhi[t, part], zero) for t in range(3)])
            else:
                sets.append([ref[x + 1, part] for ref in refs])
            if y == 0:
                before = [jnp.where(j > 0, ylo[t, x, TILE - 1:TILE], zrow) for t in range(3)]
            else:
                before = [ref[x, y - 1:y] for ref in refs]
            if y + step == width:
                after = [jnp.where(j < m - 1, yhi[t, x, 0:1], zrow) for t in range(3)]
            else:
                after = [ref[x, y + step:y + step + 1] for ref in refs]
            sets.append([jnp.where(row == 0, b, pltpu.roll(c, 1, 0)) for b, c in zip(before, center)])
            sets.append([jnp.where(row == step - 1, a, pltpu.roll(c, step - 1, 0)) for a, c in zip(after, center)])
            sets.append([jnp.where(lane == 0, 0.0, pltpu.roll(c, 1, 1)) for c in center])
            sets.append([jnp.where(lane == depth - 1, 0.0, pltpu.roll(c, depth - 1, 1)) for c in center])
            fc, oc, kc = center
            df, do = zero, zero
            for fs, os, ks in sets:
                weight = 0.5 * (kc + ks)
                df = df + weight * (fs - fc)
                do = do + weight * (os - oc)
            prod = fc * oc
            react = r_ref[x, part] * prod / jnp.sqrt(1.0 + prod * prod)
            fn_ref[x, part] = fc + 0.15 * (df - react)
            on_ref[x, part] = oc + 0.15 * (do + react)
        u = jnp.concatenate([ref[x, part] for ref in (fn_ref, on_ref) for x in range(planes)], axis=0)
        at = 0
        for a in range(0, depth, LANES):
            total = lax.dot_general(u[:, a:a + LANES], u[:, a:], dims, precision=HIGHEST, preferred_element_type=jnp.float32)
            for b in range(0, depth - a, LANES):
                block = total[:, b:b + LANES]
                held_rows = slice(at, at + LANES)
                gram[held_rows] = block if q == 0 else gram[held_rows] + block
                at += LANES
    stores = [
        pltpu.make_async_copy(src, dst, local_sem.at[t])
        for t, (src, dst) in enumerate(((fn_ref, fn_hbm), (on_ref, on_hbm)))
    ]
    for copy in stores:
        copy.start()
    gram[...] = gram[...] / rows
    if stages:
        count = len(stages)
        sum_over_all(index, stages, gram, g_out, scratch[:count], scratch[count:2 * count], scratch[2 * count:])
    else:
        g_out[...] = gram[...]
    for side in range(2):
        @pl.when(sides[2 + side][0])
        def _(side=side):
            for copy in y_copies(side):
                copy.wait_send()

        @pl.when(sides[side][0])
        def _(side=side):
            for part in range(parts):
                for copy in x_copies(side, part):
                    copy.wait_send()

    for part in range(parts):
        @pl.when(part < relayed)
        def _(part=part):
            for copy in from_relay(0, part):
                copy.wait_send()
    for copy in stores:
        copy.wait()


def update(n, m, rows, stages, fuel, oxidizer, kappa, rate):
    planes, width, depth = fuel.shape
    blocks = depth // LANES
    parts = 4 if width % (4 * TILE) == 0 else 1
    gram_rows = blocks * (blocks + 1) // 2 * LANES
    scratch = [pltpu.VMEM(fuel.shape, jnp.float32)] * 6
    scratch += [pltpu.VMEM((3, width, depth), jnp.float32)] * 2
    scratch += [pltpu.VMEM((3, planes, TILE, depth), jnp.float32)] * 2
    scratch += [pltpu.VMEM((gram_rows, LANES), jnp.float32)]
    scratch += [pltpu.VMEM((3, width, depth), jnp.float32)]
    scratch += [pltpu.SemaphoreType.DMA((4,))]
    scratch += [pltpu.SemaphoreType.DMA((2, parts, 3))] * 2
    scratch += [pltpu.SemaphoreType.DMA((2, 3))] * 2
    scratch += [pltpu.SemaphoreType.DMA((parts, 3))] * 2
    if stages:
        inbox, held, length = [], [], gram_rows
        for _, _, size in stages:
            length //= size
            inbox.append(pltpu.VMEM((size - 1, length, LANES), jnp.float32))
            held.append(pltpu.VMEM((length, LANES), jnp.float32))
        most = max(stage[2] for stage in stages)
        scratch += inbox + held + [pltpu.SemaphoreType.DMA((len(stages), most - 1))] * 4
    field = jax.ShapeDtypeStruct(fuel.shape, jnp.float32)
    any_spec = pl.BlockSpec(memory_space=pl.ANY)
    return pl.pallas_call(
        functools.partial(update_kernel, n, m, rows, parts, stages),
        out_shape=(field, field, jax.ShapeDtypeStruct((gram_rows, LANES), jnp.float32)),
        in_specs=[any_spec] * 4,
        out_specs=(any_spec, any_spec, pl.BlockSpec(memory_space=pltpu.VMEM)),
        scratch_shapes=scratch,
        compiler_params=pltpu.CompilerParams(collective_id=0, has_side_effects=True),
        name="update",
    )(fuel, oxidizer, kappa, rate)


def stacked_dot(left, right):
    dims = (((0,), (0,)), ((), ()))
    def pieces(v):
        h = v.astype(jnp.bfloat16).astype(jnp.float32)
        m = (v - h).astype(jnp.bfloat16).astype(jnp.float32)
        return h, m, v - h - m
    (a, b, c), (d, e, f) = pieces(left), pieces(right)
    lhs = jnp.concatenate([a, a, b, a, c, b], axis=0).astype(jnp.bfloat16)
    rhs = jnp.concatenate([d, e, d, f, d, e], axis=0).astype(jnp.bfloat16)
    return lax.dot_general(lhs, rhs, dims, preferred_element_type=jnp.float32)


def column_of(panel, at):
    return jnp.broadcast_to(panel[:, at:at + 1], (TILE, LANES))


def factor_kernel(group, g_ref, fn_in, on_in, r_ref, fn_out, on_out, a_ref, fn_ref, on_ref, sems):
    loads = [pltpu.make_async_copy(fn_in, fn_ref, sems.at[0]), pltpu.make_async_copy(on_in, on_ref, sems.at[1])]
    stores = [pltpu.make_async_copy(fn_ref, fn_out, sems.at[2]), pltpu.make_async_copy(on_ref, on_out, sems.at[3])]
    for copy in loads:
        copy.start()
    depth = r_ref.shape[0]
    blocks = depth // LANES
    at = 0
    for b in range(blocks):
        for c in range(b, blocks):
            a_ref[b * LANES:(b + 1) * LANES, c * LANES:(c + 1) * LANES] = g_ref[at:at + LANES]
            at += LANES
    dims = (((0,), (0,)), ((), ()))
    dot = functools.partial(lax.dot_general, dimension_numbers=dims, precision=HIGHEST, preferred_element_type=jnp.float32)
    sub = lax.broadcasted_iota(jnp.int32, (TILE, LANES), 0)
    lane = lax.broadcasted_iota(jnp.int32, (TILE, LANES), 1)
    for b in range(blocks):
        c0 = b * LANES
        tiles = range(blocks - b)
        if c0:
            r_ref[c0:c0 + LANES, :c0] = jnp.zeros((LANES, c0), jnp.float32)
        for p in range(0, LANES, TILE * group):
            before = []
            for q in range(p, p + TILE * group, TILE):
                r0 = c0 + q
                strips = [a_ref[r0:r0 + TILE, c0 + t * LANES:c0 + (t + 1) * LANES] for t in tiles]
                for s, inv, low, rows in before:
                    factors = []
                    for k in range(TILE):
                        value = column_of(strips[0], s + k)
                        for j in range(k):
                            value = value - factors[j] * low[k, j]
                        factors.append(value * inv[k])
                    for t in tiles:
                        for k in range(TILE):
                            strips[t] = strips[t] - factors[k] * rows[t][k]
                e = {}
                for k in range(TILE):
                    column = column_of(strips[0], q + k)
                    for i in range(k, TILE):
                        e[i, k] = jnp.broadcast_to(column[i:i + 1], (TILE, LANES))
                inv, low = [], {}
                for k in range(TILE):
                    inv.append(lax.rsqrt(e[k, k]))
                    for i in range(k + 1, TILE):
                        low[i, k] = e[i, k] * inv[k]
                    for j in range(k + 1, TILE):
                        for i in range(j, TILE):
                            e[i, j] = e[i, j] - low[i, k] * low[j, k]
                rows = []
                for t in tiles:
                    made = []
                    for k in range(TILE):
                        value = jnp.broadcast_to(strips[t][k:k + 1], (TILE, LANES))
                        for j in range(k):
                            value = value - low[k, j] * made[j]
                        made.append(value * inv[k])
                    rows.append(made)
                    strip = made[0]
                    for k in range(1, TILE):
                        strip = jnp.where(sub == k, made[k], strip)
                    if t == 0:
                        strip = jnp.where(lane >= sub + q, strip, 0.0)
                    r_ref[r0:r0 + TILE, c0 + t * LANES:c0 + (t + 1) * LANES] = strip
                before.append((q, inv, low, rows))
            low_end = p + TILE * group
            if low_end < LANES:
                upper = r_ref[c0 + p:c0 + low_end, c0:]
                a_ref[c0 + low_end:c0 + LANES, c0:] -= stacked_dot(upper[:, :LANES], upper)[low_end:]
        if b == 0:
            for load, store in zip(loads, stores):
                load.wait()
                store.start()
        for d in range(b + 1, blocks):
            d0 = d * LANES
            a_ref[d0:d0 + LANES, d0:] -= dot(r_ref[c0:c0 + LANES, d0:d0 + LANES], r_ref[c0:c0 + LANES, d0:])
    for copy in stores:
        copy.wait()


def factor(gram, fuel_next, oxid_next):
    depth = fuel_next.shape[2]
    field = jax.ShapeDtypeStruct(fuel_next.shape, jnp.float32)
    vmem = pl.BlockSpec(memory_space=pltpu.VMEM)
    any_spec = pl.BlockSpec(memory_space=pl.ANY)
    return pl.pallas_call(
        functools.partial(factor_kernel, 4),
        out_shape=(jax.ShapeDtypeStruct((depth, depth), jnp.float32), field, field),
        in_specs=[vmem, any_spec, any_spec],
        out_specs=(vmem, any_spec, any_spec),
        scratch_shapes=[
            pltpu.VMEM((depth, depth), jnp.float32),
            pltpu.VMEM(fuel_next.shape, jnp.float32),
            pltpu.VMEM(fuel_next.shape, jnp.float32),
            pltpu.SemaphoreType.DMA((4,)),
        ],
        name="factor",
    )(gram, fuel_next, oxid_next)


def shards(n, m, fuel, oxidizer, kappa, rate):
    planes, width, depth = fuel.shape
    rows = 2 * planes * width * n * m
    blocks = depth // LANES
    stages = ()
    if blocks * (blocks + 1) // 2 * LANES % (TILE * n * m) == 0:
        pairs = [("gy", 1, 2), ("gy", 2, 2)] if m == 4 else [("gy", 1, m)]
        stages = tuple(pairs + [("gx", 1, n)])
    fuel_next, oxid_next, gram = update(n, m, rows, stages, fuel, oxidizer, kappa, rate)
    if not stages:
        gram = lax.psum(gram, ("gx", "gy"))
    r_factor, fuel_next, oxid_next = factor(gram, fuel_next, oxid_next)
    return (fuel_next, oxid_next, r_factor)


def solution(mesh):
    spec = P("gx", "gy", None)
    body = functools.partial(shards, mesh.shape["gx"], mesh.shape["gy"])
    return jax.shard_map(body, mesh=mesh, in_specs=(spec,) * 4, out_specs=(spec, spec, P()), check_vma=False)
```

profile of v0, /device:TPU:0, one launch (start us, length us, event | category | flops | bytes accessed | tf_op | source)
XLA Modules:
  0.0 78.9 jit_solution(18381226980398563536)
XLA Ops:
  0.6 63.1 %update.1 = (f32[2,192,384]{2,1,0:T(8,128)}, f32[2,192,384]{2,1,0:T(8,128)}, f32[768,128]{1,0:T(8,128)}) custom-call(f32[2,192,384]{2,1,0:T(8,128)} %f_hbm.1, f32[2,192,384]{2,1,0:T(8,128)} %o_hbm.1, f32[2,192,384]{2,1,0:T(8,128)} %k_hbm.1, f32[2,192,384]{2,1,0:T(8,128)} %r_hbm.1), custom_call_target="tpu_custom_call" | custom-call | tf_op jit(solution)/shard_map/update/pallas_call | solution.py:334
  63.8 15.1 %factor.1 = (f32[384,384]{1,0:T(8,128)}, f32[2,192,384]{2,1,0:T(8,128)}, f32[2,192,384]{2,1,0:T(8,128)}) custom-call(f32[768,128]{1,0:T(8,128)} %get-tuple-element.9.g_ref, f32[2,192,384]{2,1,0:T(8,128)} %get-tuple-element.10.fn_in, f32[2,192,384]{2,1,0:T(8,128)} %get-tuple-element.11.on_in), custom_call_target="tpu_custom_call" | custom-call | tf_op jit(solution)/shard_map/factor/pallas_call | solution.py:446
where the time goes:
time: 79.1 us; the launch traced here: 78.9 us
  Pallas kernels  78.2 us (99%)
    pallas_call x1, Pallas kernels, update(): pl.pallas_call(functools.partial(update_kernel, n, m, rows, parts, stages...  63.1 us
    pallas_call x1, Pallas kernels, factor(): pl.pallas_call(functools.partial(factor_kernel, 4), out_shape=(jax.ShapeD...  15.1 us

commit v1 on v0

--- a/solution.py
+++ b/solution.py
@@ -11,6 +11,8 @@
 TILE = 8
 LANES = 128
 HIGHEST = lax.Precision.HIGHEST
+GROUP = 4
+AHEAD = 3
 
 
 def peer(index, stage, k):
@@ -340,6 +342,527 @@
         compiler_params=pltpu.CompilerParams(collective_id=0, has_side_effects=True),
         name="update",
     )(fuel, oxidizer, kappa, rate)
+
+
+def eliminate(a_ref, group, first, emit):
+    width = a_ref.shape[1]
+    tiles = range(width // LANES)
+    sub = lax.broadcasted_iota(jnp.int32, (TILE, LANES), 0)
+    lane = lax.broadcasted_iota(jnp.int32, (TILE, LANES), 1)
+    before, upper = [], [[] for _ in tiles]
+    for q in range(first, first + TILE * group, TILE):
+        strips = [a_ref[q:q + TILE, t * LANES:(t + 1) * LANES] for t in tiles]
+        for s, inv, low, rows in before:
+            factors = []
+            for k in range(TILE):
+                value = column_of(strips[0], s + k)
+                for j in range(k):
+                    value = value - factors[j] * low[k, j]
+                factors.append(value * inv[k])
+            for t in tiles:
+                for k in range(TILE):
+                    strips[t] = strips[t] - factors[k] * rows[t][k]
+        e = {}
+        for k in range(TILE):
+            column = column_of(strips[0], q + k)
+            for i in range(k, TILE):
+                e[i, k] = jnp.broadcast_to(column[i:i + 1], (TILE, LANES))
+        inv, low = [], {}
+        for k in range(TILE):
+            inv.append(lax.rsqrt(e[k, k]))
+            for i in range(k + 1, TILE):
+                low[i, k] = e[i, k] * inv[k]
+            for j in range(k + 1, TILE):
+                for i in range(j, TILE):
+                    e[i, j] = e[i, j] - low[i, k] * low[j, k]
+        rows = []
+        for t in tiles:
+            made = []
+            for k in range(TILE):
+                value = jnp.broadcast_to(strips[t][k:k + 1], (TILE, LANES))
+                for j in range(k):
+                    value = value - low[k, j] * made[j]
+                made.append(value * inv[k])
+            rows.append(made)
+            strip = made[0]
+            for k in range(1, TILE):
+                strip = jnp.where(sub == k, made[k], strip)
+            if t == 0:
+                strip = jnp.where(lane >= sub + q, strip, 0.0)
+            emit(q, t, strip)
+            upper[t].append(strip)
+        before.append((q, inv, low, rows))
+    end = first + TILE * group
+    if end < LANES:
+        done = jnp.concatenate([jnp.concatenate(u, axis=0) for u in upper], axis=1)
+        a_ref[end:, :] -= stacked_dot(done[:, :LANES], done)[end:]
+
+
+def early_kernel(
+    n, m, rows, parts,
+    f_hbm, o_hbm, k_hbm, r_hbm, fn_hbm, on_hbm, g_out, w_out, rp_out,
+    f_ref, o_ref, k_ref, r_ref, fn_ref, on_ref, xlo, xhi, ylo, yhi, passing,
+    local_sem, xs_sem, xr_sem, ys_sem, yr_sem, ps_sem, pr_sem, as_sem, ar_sem, *scratch
+):
+    i, j = lax.axis_index("gx"), lax.axis_index("gy")
+    index = {"gx": i, "gy": j}
+    planes, width, depth = f_ref.shape
+    blocks = depth // LANES
+    scratch = list(scratch)
+    take = lambda count: [scratch.pop(0) for _ in range(count)]
+    grams, inbox, held, inbox_x, held_x, inbox_z = (take(blocks) for _ in range(6))
+    totals = take(blocks - 1) + [g_out]
+    panels = take(blocks - 1)
+    step = width // parts
+    sides = (
+        (i < n - 1, i > 0, i + 1, j),
+        (i > 0, i < n - 1, i - 1, j),
+        (j < m - 1, j > 0, i, j + 1),
+        (j > 0, j < m - 1, i, j - 1),
+    )
+    z, odd, depth_z = i // 2, lax.rem(i, 2) == 1, n // 2
+    rising = lambda pair: (pair + 1) * parts // depth_z
+    falling = lambda pair: (depth_z - 1 - pair) * parts // depth_z
+    if n % 2 or n < 4:
+        indirect = (0, 0)
+        relayed = 0
+    else:
+        indirect = (jnp.where(odd, falling(z), 0), jnp.where(odd, 0, rising(z - 1)))
+        relayed = jnp.where(odd, rising(z - 1), falling(z))
+    via = (i - 1, i + 1)
+    onward = jnp.where(odd, i - 2, i + 2)
+    lands = (jnp.logical_not(odd), odd)
+    relayed = jnp.where(odd, jnp.where(z > 0, relayed, 0), jnp.where(z < depth_z - 1, relayed, 0))
+    loads = [
+        pltpu.make_async_copy(src, dst, local_sem.at[t])
+        for t, (src, dst) in enumerate(((f_hbm, f_ref), (o_hbm, o_ref), (k_hbm, k_ref), (r_hbm, r_ref)))
+    ]
+    for copy in loads:
+        copy.start()
+    core, along = ("gy", 1, 2), ("gx", 2, n // 2)
+    ring = [(i, peer(index, core, 1)[2][1])]
+    ring += [peer(index, along, k)[2] for k in range(1, n // 2)]
+    corners = [(i, peer(index, ("gy", 2, 2), 1)[2][1]), (peer(index, ("gx", 1, 2), 1)[2][0], j)]
+    corners.append((corners[1][0], corners[0][1]))
+    greets = sides + ((i < n - 2, None, i + 2, j), (i > 1, None, i - 2, j))
+    barrier = pltpu.get_barrier_semaphore()
+    greeted = sum(has.astype(jnp.int32) for has, _, _, _ in greets)
+    for has, _, a, b in greets:
+        @pl.when(has)
+        def _(a=a, b=b):
+            pl.semaphore_signal(barrier, inc=1, device_id=(a, b), device_id_type=MESH)
+    for device in ring + corners:
+        pl.semaphore_signal(barrier, inc=1, device_id=device, device_id_type=MESH)
+        greeted = greeted + 1
+    with jax.named_scope("barrier"):
+        pl.semaphore_wait(barrier, greeted)
+    fields = (f_hbm, o_hbm, k_hbm)
+
+    def cut(at):
+        c, q = divmod(at, parts)
+        return pl.ds(q * step, step), pl.ds(c * LANES, LANES)
+
+    def x_copies(side, at):
+        _, _, a, b = sides[side]
+        return [
+            pltpu.make_async_remote_copy(
+                src_ref=ref.at[((planes - 1, 0)[side],) + cut(at)],
+                dst_ref=(xlo, xhi)[side].at[(t,) + cut(at)],
+                send_sem=xs_sem.at[side],
+                recv_sem=xr_sem.at[side, at],
+                device_id=(a, b),
+                device_id_type=MESH,
+            )
+            for t, ref in enumerate(fields)
+        ]
+
+    def to_relay(side, at):
+        return [
+            pltpu.make_async_remote_copy(
+                src_ref=ref.at[((planes - 1, 0)[side],) + cut(at)],
+                dst_ref=passing.at[(t,) + cut(at)],
+                send_sem=xs_sem.at[side],
+                recv_sem=pr_sem.at[at],
+                device_id=(via[side], j),
+                device_id_type=MESH,
+            )
+            for t, ref in enumerate(fields)
+        ]
+
+    def from_relay(side, at):
+        return [
+            pltpu.make_async_remote_copy(
+                src_ref=passing.at[(t,) + cut(at)],
+                dst_ref=(xlo, xhi)[side].at[(t,) + cut(at)],
+                send_sem=ps_sem.at[0],
+                recv_sem=xr_sem.at[side, at],
+                device_id=(onward, j),
+                device_id_type=MESH,
+            )
+            for t in range(3)
+        ]
+
+    def y_copies(side):
+        _, _, a, b = sides[2 + side]
+        return [
+            pltpu.make_async_remote_copy(
+                src_ref=ref.at[:, pl.ds((width - TILE, 0)[side], TILE)],
+                dst_ref=(ylo, yhi)[side].at[t],
+                send_sem=ys_sem.at[side],
+                recv_sem=yr_sem.at[side],
+                device_id=(a, b),
+                device_id_type=MESH,
+            )
+            for t, ref in enumerate(fields)
+        ]
+
+    def whole(ref, send, recv, device=None):
+        return pltpu.make_async_remote_copy(
+            src_ref=ref, dst_ref=ref, send_sem=send, recv_sem=recv, device_id=device or (i, j), device_id_type=MESH
+        )
+
+    def post(at):
+        q = at % parts
+        for side in range(2):
+            @pl.when(sides[side][0] & (q >= indirect[side]))
+            def _(side=side):
+                for copy in x_copies(side, at):
+                    copy.start()
+
+            @pl.when(sides[side][0] & (q < indirect[side]))
+            def _(side=side):
+                for copy in to_relay(side, at):
+                    copy.start()
+
+    row = lax.broadcasted_iota(jnp.int32, (step, LANES), 0)
+    lane = lax.broadcasted_iota(jnp.int32, (step, LANES), 1)
+    refs = (f_ref, o_ref, k_ref)
+    zero = jnp.zeros((step, LANES), jnp.float32)
+    zrow = jnp.zeros((1, LANES), jnp.float32)
+    columns = (((0,), (0,)), ((), ()))
+    products = (((1,), (0,)), ((), ()))
+
+    def dot(left, right, dims):
+        return lax.dot_general(left, right, dims, precision=HIGHEST, preferred_element_type=jnp.float32)
+
+    def arrive(at):
+        q = at % parts
+        @pl.when(q < relayed)
+        def _():
+            whole(passing.at[(slice(None),) + cut(at)], ps_sem.at[0], pr_sem.at[at]).wait_recv()
+
+        for side in range(2):
+            @pl.when((q < relayed) & lands[side])
+            def _(side=side):
+                for copy in from_relay(side, at):
+                    copy.start()
+
+        for side in range(2):
+            @pl.when(sides[side][1])
+            def _(side=side):
+                whole((xlo, xhi)[side].at[(slice(None),) + cut(at)], xs_sem.at[side], xr_sem.at[side, at]).wait_recv()
+
+    def advance(at):
+        c, q = divmod(at, parts)
+        y = q * step
+        here = cut(at)
+        cols = here[1]
+        for x in range(planes):
+            center = [ref[(x,) + here] for ref in refs]
+            sets = []
+            if x == 0:
+                sets.append([jnp.where(i > 0, xlo[(t,) + here], zero) for t in range(3)])
+            else:
+                sets.append([ref[(x - 1,) + here] for ref in refs])
+            if x == planes - 1:
+                sets.append([jnp.where(i < n - 1, xhi[(t,) + here], zero) for t in range(3)])
+            else:
+                sets.append([ref[(x + 1,) + here] for ref in refs])
+            if y == 0:
+                before = [jnp.where(j > 0, ylo[t, x, TILE - 1:TILE, cols], zrow) for t in range(3)]
+            else:
+                before = [ref[x, y - 1:y, cols] for ref in refs]
+            if y + step == width:
+                after = [jnp.where(j < m - 1, yhi[t, x, 0:1, cols], zrow) for t in range(3)]
+            else:
+                after = [ref[x, y + step:y + step + 1, cols] for ref in refs]
+            sets.append([jnp.where(row == 0, b, pltpu.roll(v, 1, 0)) for b, v in zip(before, center)])
+            sets.append([jnp.where(row == step - 1, a, pltpu.roll(v, step - 1, 0)) for a, v in zip(after, center)])
+            if c:
+                left = [pltpu.roll(ref[x, here[0], pl.ds((c - 1) * LANES, LANES)], 1, 1) for ref in refs]
+            else:
+                left = [zero] * 3
+            if c < blocks - 1:
+                right = [pltpu.roll(ref[x, here[0], pl.ds((c + 1) * LANES, LANES)], LANES - 1, 1) for ref in refs]
+            else:
+                right = [zero] * 3
+            sets.append([jnp.where(lane == 0, b, pltpu.roll(v, 1, 1)) for b, v in zip(left, center)])
+            sets.append([jnp.where(lane == LANES - 1, a, pltpu.roll(v, LANES - 1, 1)) for a, v in zip(right, center)])
+            fc, oc, kc = center
+            df, do = zero, zero
+            for fs, os, ks in sets:
+                weight = 0.5 * (kc + ks)
+                df = df + weight * (fs - fc)
+                do = do + weight * (os - oc)
+            prod = fc * oc
+            react = r_ref[(x,) + here] * prod / jnp.sqrt(1.0 + prod * prod)
+            fn_ref[(x,) + here] = fc + 0.15 * (df - react)
+            on_ref[(x,) + here] = oc + 0.15 * (do + react)
+        to = (c + 1) * LANES
+        u = jnp.concatenate([ref[x, here[0], :to] for ref in (fn_ref, on_ref) for x in range(planes)], axis=0)
+        total = dot(u, u[:, c * LANES:], columns)
+        grams[c][...] = total if q == 0 else grams[c][...] + total
+
+    def sends(c, s, source, target, devices):
+        return [
+            pltpu.make_async_remote_copy(
+                src_ref=source(*to),
+                dst_ref=target(*to),
+                send_sem=as_sem.at[c, s],
+                recv_sem=ar_sem.at[c, s],
+                device_id=device,
+                device_id_type=MESH,
+            )
+            for to, device in devices
+        ]
+
+    def span(at, length):
+        return pl.ds(pl.multiple_of(at * length, TILE), length)
+
+    half = [(c + 1) * LANES // 2 for c in range(blocks)]
+    piece = [length // (n // 2) for length in half]
+    mine_core, mine_along = lax.rem(j, 2), i // 2
+    beside = [((1 - mine_core, 0), ring[0])]
+    others = [((lax.rem(mine_along + k, n // 2), k - 1), ring[k]) for k in range(1, n // 2)]
+    around = [((0, k), corners[k]) for k in range(3)]
+
+    def whole_slot(c):
+        start = mine_core * half[c] + mine_along * piece[c]
+        return pl.ds(pl.multiple_of(start, TILE), piece[c])
+
+    def exchange(c, s):
+        if s == 0:
+            return sends(c, 0, lambda a, k: grams[c].at[span(a, half[c])], lambda a, k: inbox[c], beside)
+        if s == 1:
+            return sends(c, 1, lambda a, k: held[c].at[span(a, piece[c])], lambda a, k: inbox_x[c].at[k], others)
+        if s == 2:
+            return sends(c, 2, lambda a, k: held_x[c], lambda a, k: inbox_z[c].at[k], around)
+        if s == 3:
+            slot = whole_slot(c)
+            return sends(c, 3, lambda a, k: totals[c].at[slot], lambda a, k: totals[c].at[slot], others)
+        part = span(mine_core, half[c])
+        return sends(c, 4, lambda a, k: totals[c].at[part], lambda a, k: totals[c].at[part], beside)
+
+    def landed(c, s):
+        region = (inbox[c], inbox_x[c], inbox_z[c], inbox_x[c], inbox[c])[s]
+        return whole(region, as_sem.at[c, s], ar_sem.at[c, s])
+
+    def reduce_step(c, s):
+        if s:
+            landed(c, s - 1).wait_recv()
+        if s == 1:
+            held[c][...] = grams[c][span(mine_core, half[c])] + inbox[c][...]
+        if s == 2:
+            total = held[c][span(mine_along, piece[c])]
+            for k in range(n // 2 - 1):
+                total = total + inbox_x[c][k]
+            held_x[c][...] = total
+        if s == 3:
+            total = (held_x[c][...] + inbox_z[c][0]) + (inbox_z[c][1] + inbox_z[c][2])
+            totals[c][whole_slot(c)] = total / rows
+        if s < 5:
+            for copy in exchange(c, s):
+                copy.start()
+
+    eye = jnp.where(
+        lax.broadcasted_iota(jnp.int32, (LANES, LANES), 0) == lax.broadcasted_iota(jnp.int32, (LANES, LANES), 1), 1.0, 0.0
+    )
+
+    def prepare(b):
+        c0 = b * LANES
+        panel, total = panels[b], totals[b]
+        s = total[c0:c0 + LANES]
+        if b:
+            above = dot(w_out[:c0, :c0], total[:c0], products)
+            rp_out[:c0, c0:c0 + LANES] = above
+            s = s - dot(above, above, columns)
+            panel[:, LANES:c0 + LANES] = -dot(above, w_out[:c0, :c0], columns)
+        panel[:, :LANES] = s
+        panel[:, c0 + LANES:] = eye
+        if c0:
+            rp_out[c0:c0 + LANES, :c0] = jnp.zeros((LANES, c0), jnp.float32)
+        rest = w_out.shape[1] - c0 - LANES
+        if rest:
+            w_out[c0:c0 + LANES, c0 + LANES:] = jnp.zeros((LANES, rest), jnp.float32)
+
+    def pivot(b, g):
+        c0 = b * LANES
+
+        def emit(q, t, strip):
+            at = slice(c0 + q, c0 + q + TILE)
+            if t == 0:
+                rp_out[at, c0:c0 + LANES] = strip
+            else:
+                w_out[at, (t - 1) * LANES:t * LANES] = strip
+
+        eliminate(panels[b], GROUP, g * GROUP * TILE, emit)
+
+    steps = blocks * parts
+    groups = LANES // (TILE * GROUP)
+    R = lambda c, s: functools.partial(reduce_step, c, s)
+    prep = lambda b: functools.partial(prepare, b)
+    C = lambda b, g: functools.partial(pivot, b, g)
+    plan = {}
+    if blocks == 3 and parts == 4 and groups == 4:
+        plan = {
+            3: [R(0, 0)], 4: [R(0, 1)], 6: [R(0, 2)], 7: [R(1, 0)], 8: [R(1, 1)], 9: [R(0, 3)], 10: [R(1, 2)],
+            11: [
+                R(2, 0), R(0, 4), R(1, 3), R(2, 1), R(0, 5), prep(0), C(0, 0), C(0, 1), C(0, 2), R(1, 4), R(2, 2), C(0, 3),
+                R(1, 5), prep(1), C(1, 0), R(2, 3), C(1, 1), C(1, 2), C(1, 3), R(2, 4), R(2, 5),
+            ],
+        }
+    else:
+        last = []
+        for c in range(blocks):
+            last += [R(c, s) for s in range(6)]
+            if c < blocks - 1:
+                last += [prep(c)] + [C(c, g) for g in range(groups)]
+        plan = {steps - 1: last}
+    for side in range(2):
+        @pl.when(sides[2 + side][0])
+        def _(side=side):
+            for copy in y_copies(side):
+                copy.start()
+    for at in range(min(AHEAD, steps)):
+        post(at)
+    for copy in loads:
+        copy.wait()
+    for side in range(2):
+        @pl.when(sides[2 + side][1])
+        def _(side=side):
+            whole((ylo, yhi)[side], ys_sem.at[side], yr_sem.at[side]).wait_recv()
+    stores = [
+        pltpu.make_async_copy(src, dst, local_sem.at[t])
+        for t, (src, dst) in enumerate(((fn_ref, fn_hbm), (on_ref, on_hbm)))
+    ]
+    for at in range(steps):
+        with jax.named_scope(f"w{at}"):
+            arrive(at)
+        if at + AHEAD < steps:
+            post(at + AHEAD)
+        with jax.named_scope(f"s{at}"):
+            advance(at)
+        for task in plan.get(at, []):
+            name = {"reduce_step": "R", "prepare": "P", "pivot": "C"}[task.func.__name__]
+            with jax.named_scope(name + "".join(map(str, task.args))):
+                task()
+            if at == steps - 1 and task is plan[at][0]:
+                for copy in stores:
+                    copy.start()
+    with jax.named_scope("sends"):
+        for c in range(blocks):
+            for s in range(5):
+                landed(c, s).wait_send()
+        for side in range(2):
+            @pl.when(sides[2 + side][0])
+            def _(side=side):
+                whole((ylo, yhi)[side], ys_sem.at[side], yr_sem.at[side]).wait_send()
+
+            @pl.when(sides[side][0])
+            def _(side=side):
+                whole((xlo, xhi)[side], xs_sem.at[side], xr_sem.at[side, 0]).wait_send()
+
+        for count in range(1, parts):
+            @pl.when(relayed == count)
+            def _(count=count):
+                whole(passing.at[:, pl.ds(0, count * step)], ps_sem.at[0], pr_sem.at[0]).wait_send()
+        for copy in stores:
+            copy.wait()
+
+
+def early(n, m, rows, fuel, oxidizer, kappa, rate):
+    planes, width, depth = fuel.shape
+    blocks = depth // LANES
+    parts = 4 if width % (4 * TILE) == 0 else 1
+    steps = blocks * parts
+    size = [(c + 1) * LANES for c in range(blocks)]
+    vmem = lambda *shape: pltpu.VMEM(shape, jnp.float32)
+    inner = depth - LANES
+    scratch = [vmem(*fuel.shape)] * 6
+    scratch += [vmem(3, width, depth)] * 2
+    scratch += [vmem(3, planes, TILE, depth)] * 2
+    scratch += [vmem(3, width, depth)]
+    scratch += [pltpu.SemaphoreType.DMA((4,))]
+    scratch += [pltpu.SemaphoreType.DMA((2,)), pltpu.SemaphoreType.DMA((2, steps))]
+    scratch += [pltpu.SemaphoreType.DMA((2,))] * 2
+    scratch += [pltpu.SemaphoreType.DMA((1,)), pltpu.SemaphoreType.DMA((steps,))]
+    scratch += [pltpu.SemaphoreType.DMA((blocks, 5))] * 2
+    scratch += [vmem(length, LANES) for length in size]
+    scratch += [vmem(length // 2, LANES) for length in size] * 2
+    scratch += [vmem(n // 2 - 1, length // n, LANES) for length in size]
+    scratch += [vmem(length // n, LANES) for length in size]
+    scratch += [vmem(3, length // n, LANES) for length in size]
+    scratch += [vmem(length, LANES) for length in size[:-1]]
+    scratch += [vmem(LANES, (b + 2) * LANES) for b in range(blocks - 1)]
+    field = jax.ShapeDtypeStruct(fuel.shape, jnp.float32)
+    any_spec = pl.BlockSpec(memory_space=pl.ANY)
+    vmem_spec = pl.BlockSpec(memory_space=pltpu.VMEM)
+    return pl.pallas_call(
+        functools.partial(early_kernel, n, m, rows, parts),
+        out_shape=(field, field, vmem(depth, LANES), vmem(inner, inner), vmem(inner, inner)),
+        in_specs=[any_spec] * 4,
+        out_specs=(any_spec, any_spec, vmem_spec, vmem_spec, vmem_spec),
+        scratch_shapes=scratch,
+        compiler_params=pltpu.CompilerParams(collective_id=0, has_side_effects=True),
+        name="early",
+    )(fuel, oxidizer, kappa, rate)
+
+
+def finish_kernel(g_ref, w_ref, rp_ref, fn_in, on_in, r_ref, fn_out, on_out, a_ref, fn_ref, on_ref, sems):
+    loads = [pltpu.make_async_copy(fn_in, fn_ref, sems.at[0]), pltpu.make_async_copy(on_in, on_ref, sems.at[1])]
+    stores = [pltpu.make_async_copy(fn_ref, fn_out, sems.at[2]), pltpu.make_async_copy(on_ref, on_out, sems.at[3])]
+    for copy in loads:
+        copy.start()
+    inner = w_ref.shape[0]
+    dot = functools.partial(lax.dot_general, precision=HIGHEST, preferred_element_type=jnp.float32)
+    above = dot(w_ref[...], g_ref[:inner], (((1,), (0,)), ((), ())))
+    a_ref[...] = g_ref[inner:] - dot(above, above, (((0,), (0,)), ((), ())))
+    r_ref[:inner, :inner] = rp_ref[...]
+    r_ref[:inner, inner:] = above
+    r_ref[inner:, :inner] = jnp.zeros((LANES, inner), jnp.float32)
+
+    def emit(q, t, strip):
+        r_ref[inner + q:inner + q + TILE, inner:] = strip
+
+    for first in range(0, LANES, GROUP * TILE):
+        eliminate(a_ref, GROUP, first, emit)
+        if first == 0:
+            for load, store in zip(loads, stores):
+                load.wait()
+                store.start()
+    for copy in stores:
+        copy.wait()
+
+
+def finish(gram, inverse, upper, fuel_next, oxid_next):
+    depth = fuel_next.shape[2]
+    field = jax.ShapeDtypeStruct(fuel_next.shape, jnp.float32)
+    vmem = pl.BlockSpec(memory_space=pltpu.VMEM)
+    any_spec = pl.BlockSpec(memory_space=pl.ANY)
+    gram, inverse, upper = (pltpu.with_memory_space_constraint(v, pltpu.VMEM) for v in (gram, inverse, upper))
+    return pl.pallas_call(
+        finish_kernel,
+        out_shape=(jax.ShapeDtypeStruct((depth, depth), jnp.float32), field, field),
+        in_specs=[vmem, vmem, vmem, any_spec, any_spec],
+        out_specs=(vmem, any_spec, any_spec),
+        scratch_shapes=[
+            pltpu.VMEM((LANES, LANES), jnp.float32),
+            pltpu.VMEM(fuel_next.shape, jnp.float32),
+            pltpu.VMEM(fuel_next.shape, jnp.float32),
+            pltpu.SemaphoreType.DMA((4,)),
+        ],
+        name="finish",
+    )(gram, inverse, upper, fuel_next, oxid_next)
 
 
 def stacked_dot(left, right):
@@ -462,13 +985,12 @@
     planes, width, depth = fuel.shape
     rows = 2 * planes * width * n * m
     blocks = depth // LANES
-    stages = ()
-    if blocks * (blocks + 1) // 2 * LANES % (TILE * n * m) == 0:
-        pairs = [("gy", 1, 2), ("gy", 2, 2)] if m == 4 else [("gy", 1, m)]
-        stages = tuple(pairs + [("gx", 1, n)])
-    fuel_next, oxid_next, gram = update(n, m, rows, stages, fuel, oxidizer, kappa, rate)
-    if not stages:
-        gram = lax.psum(gram, ("gx", "gy"))
+    if blocks > 1 and m == 4 and n % 2 == 0 and n >= 4 and LANES % (TILE * n) == 0:
+        fuel_next, oxid_next, gram, inverse, upper = early(n, m, rows, fuel, oxidizer, kappa, rate)
+        r_factor, fuel_next, oxid_next = finish(gram, inverse, upper, fuel_next, oxid_next)
+        return (fuel_next, oxid_next, r_factor)
+    fuel_next, oxid_next, gram = update(n, m, rows, (), fuel, oxidizer, kappa, rate)
+    gram = lax.psum(gram, ("gx", "gy"))
     r_factor, fuel_next, oxid_next = factor(gram, fuel_next, oxid_next)
     return (fuel_next, oxid_next, r_factor)
 

time: 79.1 us -> 68.5 us (0.87)
  Pallas kernels: 78.2 us -> 67.5 us
    pallas_call x2, Pallas kernels: 78.2 us -> 67.5 us  [the longest x1 61 us: early(): pl.pallas_call(functools.partial(early_kernel, n, m, rows, parts), out_sh...]
where the time goes in v1:
time: 68.5 us; the launch traced here: 68.3 us
  Pallas kernels  67.5 us (99%)
  between operations  0.8 us (1%)
    pallas_call x1, Pallas kernels, early(): pl.pallas_call(functools.partial(early_kernel, n, m, rows, parts), out_sh...  61 us
    pallas_call x1, Pallas kernels, finish(): pl.pallas_call(finish_kernel, out_shape=(jax.ShapeDtypeStruct((depth, dep...  6.48 us

profile of v1, /device:TPU:0, one launch (start us, length us, event | category | flops | bytes accessed | tf_op | source)
XLA Modules:
  0.0 68.3 jit_solution(5656145786497186775)
XLA Ops:
  0.6 61.0 %early.1 = (f32[2,192,384]{2,1,0:T(8,128)}, f32[2,192,384]{2,1,0:T(8,128)}, f32[384,128]{1,0:T(8,128)S(1)}, f32[256,256]{1,0:T(8,128)S(1)}, f32[256,256]{1,0:T(8,128)S(1)}) custom-call(f32[2,192,384]{2,1,0:T(8,128)} %f_hbm.1, f32[2,192,384]{2,1,0:T(8,128)} %o_hbm.1, f32[2,192,384]{2,1,0:T(8,128)} %k_hbm.1, f32[2,192,384]{2,1,0:T(8,128)} %r_hbm.1), custom_call_target="tpu_custom_call" | custom-call | tf_op jit(solution)/shard_map/early/pallas_call | solution.py:810
  61.7 6.5 %finish.1 = (f32[384,384]{1,0:T(8,128)}, f32[2,192,384]{2,1,0:T(8,128)}, f32[2,192,384]{2,1,0:T(8,128)}) custom-call(f32[384,128]{1,0:T(8,128)S(1)} %get-tuple-element.11.g_ref, f32[256,256]{1,0:T(8,128)S(1)} %get-tuple-element.12.w_ref, f32[256,256]{1,0:T(8,128)S(1)} %get-tuple-element.13.rp_ref, f32[2,192,384]{2,1,0:T(8,128)} %get-tuple-element.14.fn_in, ...), custom_call_target="tpu_custom_call" | custom-call | tf_op jit(solution)/shard_map/finish/pallas_call | solution.py:853
